TPU v7x, 256 devices: a whole 4x4x8 slice. The times are simulated.
256 devices in a mesh: clu: 32 (over x, y, core), sub: 8 (over z).
Axes of the slice: x: 4, y: 4, z: 8, core: 2. Of those that a mesh axis runs over, the one named last changes fastest.
Arguments:
- load_cases: float32 [128, 393216], P(None, ('clu', 'sub')), may hold values from -90 to 90
- initial: float32 [128, 393216], P(None, ('clu', 'sub')), may hold values from -6 to 6
- dual_blocks: bfloat16 [393216, 1536], P(('clu', 'sub')), may hold values from -1 to 3, as said below
- dirichlet: bfloat16 [393216, 1536], P(('clu', 'sub')), may hold values from -1 to 3, as said below
- rigid_modes: float32 [16384, 1536], P(('clu', 'sub')), may hold values from -1 to 1
- coarse_inverse: float32 [16384, 512], P(('clu', 'sub')), may hold values from -2 to 2, as said below
- face_block: int32 [256, 12], P(('clu', 'sub')), may hold values from 0 to 11, each once within a row
- active: int32 [256, 4], P(('clu', 'sub')), may hold values from 0 to 1, as said below
- membership: int32 [256], P('clu'), may hold values from 0 to 1
Outputs:
- multipliers: float32 [128, 393216], P(None, ('clu', 'sub'))
- residual: float32 [128, 393216], P(None, ('clu', 'sub'))
Inputs may be any that keep to these rules, and one draw needn't show every extreme that they name: active[s, g] equals active[p, g] for the partner p of subdomain s in colour g. `coarse_inverse`: each cluster's 512 rows form the inverse of the symmetric positive definite matrix C C^T + 0.5 I, where C stacks the rigid_modes rows of the cluster's subdomains. `dual_blocks`: each subdomain's block is symmetric. `dirichlet`: each subdomain's block is symmetric.
All inputs are finite; a program needn't handle non-finite values.
Results may differ from a plain program's by a relative error of at most 0.0022.
Values sent between devices are 32-bit elements; how exact they have to be, the bound alone decides.
No kernel may reach another device: no remote copies, remote signals or barrier semaphores. Data moves between devices by JAX's collectives and lax.ppermute only.
A program may use at most 64 MiB of HBM per device.

v0:
```python
import jax
import jax.numpy as jnp
from jax import lax
from jax.sharding import PartitionSpec as P

BLK = 128
E = 64
NCOL = 4
ITERS = 3
HIGH = lax.Precision.HIGHEST


def from_partner(value, axis, bit):
    mask = 2**bit
    pairs = [(source, source ^ mask) for source in range(lax.axis_size(axis))]
    return lax.ppermute(value, axis, pairs)


def on_device(
    load_cases,
    initial,
    dual_blocks,
    dirichlet,
    rigid_modes,
    coarse_inverse,
    face_block,
    active,
    membership,
):
    cases = load_cases.shape[0]
    blocks = dual_blocks.shape[0] // BLK
    per_colour = blocks // NCOL
    onehot = (face_block[0][:, None] == jnp.arange(blocks)[None, :]).astype(jnp.float32)
    edge_gates = active[0].astype(jnp.float32)
    own_index = lax.axis_index("sub")
    my_group = lax.dynamic_slice_in_dim(membership, own_index, 1)[0]
    same_group = (membership == my_group).astype(jnp.float32)

    def apply_local(vector, matrix):
        return jnp.dot(vector.astype(jnp.bfloat16), matrix, preferred_element_type=jnp.float32)

    def assemble(product):
        blocked = product.reshape(cases, blocks, BLK)
        slot_vals = jnp.einsum("jq,kqb->kjb", onehot, blocked, precision=HIGH)
        received = []
        for colour in range(NCOL - 1):
            outgoing = slot_vals[:, colour * per_colour : (colour + 1) * per_colour, :]
            incoming = from_partner(outgoing, "clu", colour)
            received.append(incoming * edge_gates[colour])
        outgoing_last = slot_vals[:, (NCOL - 1) * per_colour :, :]
        incoming_last = from_partner(outgoing_last, "sub", 0)
        received.append(incoming_last * edge_gates[NCOL - 1])
        joined = jnp.concatenate(received, axis=1)
        added = jnp.einsum("jq,kjb->kqb", onehot, joined, precision=HIGH)
        return product + added.reshape(cases, blocks * BLK)

    def coarse(vector):
        coeffs = jnp.einsum("em,km->ek", rigid_modes, vector, precision=HIGH)
        flat = coeffs.reshape(1, E * cases)
        piece = lax.all_gather(flat, "sub", axis=0, tiled=True)
        count = piece.shape[0]
        masked = (piece.reshape(count, E, cases) * same_group[:, None, None]).reshape(
            count * E, cases
        )
        amounts = jnp.dot(coarse_inverse, masked, precision=HIGH)
        correction = jnp.einsum("ek,em->km", amounts, rigid_modes, precision=HIGH)
        return vector - correction

    residual = coarse(load_cases - assemble(apply_local(initial, dual_blocks)))
    multipliers = initial
    for step in range(ITERS):
        search = coarse(assemble(apply_local(residual, dirichlet)))
        image = coarse(assemble(apply_local(search, dual_blocks)))
        cross_sum = jnp.sum(residual * image, axis=1)
        image_sum = jnp.sum(image * image, axis=1)
        cross_all, image_all = lax.psum((cross_sum, image_sum), ("clu", "sub"))
        step_len = cross_all / (image_all + 1e-06)
        multipliers = multipliers + step_len[:, None] * search
        residual = residual - step_len[:, None] * image
    return (multipliers, residual)


def solution(mesh):
    in_specs = (
        P(None, ("clu", "sub")),
        P(None, ("clu", "sub")),
        P(("clu", "sub"), None),
        P(("clu", "sub"), None),
        P(("clu", "sub"), None),
        P(("clu", "sub"), None),
        P(("clu", "sub"), None),
        P(("clu", "sub"), None),
        P("clu"),
    )
    out_specs = (P(None, ("clu", "sub")), P(None, ("clu", "sub")))
    return jax.shard_map(
        on_device, mesh=mesh, in_specs=in_specs, out_specs=out_specs, check_vma=False
    )
```

profile of v0, /device:TPU:1, one launch (start us, length us, event | category | flops | bytes accessed | tf_op | source)
XLA Modules:
  0.0 650.1 jit_solution(13790412827187783038)
XLA Ops:
  0.7 3.4 fusion.61
  5.7 3.3 collective-permute-start
  9.0 2.8 collective-permute-start.2
  18.8 5.1 collective-permute-done.1
  28.3 2.1 fusion.120
  30.4 22.0 %all-gather = f32[8,1,8192]{2,1,0:T(1,128)S(1)} all-gather(f32[1,1,8192]{2,1,0:T(1,128)S(1)} %bitcast.168), channel_id=1, replica_groups=mesh['clu'=32,'sub'=8] {'sub'}, dimensions={0}, use_global_device_ids=true | all-gather | bytes 294912 | tf_op jit(solution)/shard_map/all_gather | solution.py:60
  52.7 2.1 convolution_subtract_fusion.6
  54.8 3.1 fusion.59
  59.6 1.8 convolution_bitcast_fusion.11
  61.6 7.0 %collective-permute-start.4 = (f32[128,3,128]{2,1,0:T(4,128)S(1)}, f32[128,3,128]{2,1,0:T(4,128)S(1)}, u32[]{:S(2)}, u32[]{:S(2)}) collective-permute-start(f32[128,3,128]{2,1,0:T(4,128)S(1)} %get-tuple-element.34), channel_id=1, source_target_pairs={{0,8},{8,0},{16,24},{24,16},{32,40},{40,32},{48,56},{56,48},{64,72... | collective-permute-start | bytes 589832 | tf_op jit(solution)/shard_map/ppermute | solution.py:16
  71.9 4.5 collective-permute-done.7
  79.0 3.3 collective-permute-done.5
  83.1 2.1 convolution_bitcast_fusion.10
  90.0 19.1 %all-gather.1 = f32[8,1,8192]{2,1,0:T(1,128)S(1)} all-gather(f32[1,1,8192]{2,1,0:T(1,128)S(1)} %bitcast.169), channel_id=1, replica_groups=mesh['clu'=32,'sub'=8] {'sub'}, dimensions={0}, use_global_device_ids=true | all-gather | bytes 294912 | tf_op jit(solution)/shard_map/all_gather | solution.py:60
  110.3 3.1 fusion.57
  114.6 2.5 copy.64
  119.2 6.9 %collective-permute-start.8 = (f32[128,3,128]{2,1,0:T(4,128)S(1)}, f32[128,3,128]{2,1,0:T(4,128)S(1)}, u32[]{:S(2)}, u32[]{:S(2)}) collective-permute-start(f32[128,3,128]{2,1,0:T(4,128)S(1)} %get-tuple-element.30), channel_id=1, source_target_pairs={{0,8},{8,0},{16,24},{24,16},{32,40},{40,32},{48,56},{56,48},{64,72... | collective-permute-start | bytes 589832 | tf_op jit(solution)/shard_map/ppermute | solution.py:16
  126.1 3.5 collective-permute-start.10
  130.3 3.5 collective-permute-done.11
  136.5 3.9 collective-permute-done.9
  141.2 2.1 convolution_bitcast_fusion.8
  143.2 2.4 copy.66
  145.6 2.3 copy.67
  150.1 18.5 %all-gather.2 = f32[8,1,8192]{2,1,0:T(1,128)S(1)} all-gather(f32[1,1,8192]{2,1,0:T(1,128)S(1)} %bitcast.170), channel_id=1, replica_groups=mesh['clu'=32,'sub'=8] {'sub'}, dimensions={0}, use_global_device_ids=true | all-gather | bytes 294912 | tf_op jit(solution)/shard_map/all_gather | solution.py:60
  170.8 81.3 %all-reduce.2 = (f32[128]{0:T(128)S(1)}, f32[128]{0:T(128)S(1)}) all-reduce(f32[128]{0:T(128)S(1)} %get-tuple-element.7, f32[128]{0:T(128)S(1)} %get-tuple-element.6), channel_id=1, replica_groups=mesh['clu'=32,'sub'=8] {'clu','sub'}, use_global_device_ids=true, to_apply=%region_1.0 | all-reduce | flops 256 | bytes 2048 | tf_op jit(solution)/shard_map/psum | solution.py:76
  253.4 3.1 fusion.55
  257.6 2.5 copy.69
  267.4 3.4 collective-permute-done.15
  273.9 4.4 collective-permute-done.13
  279.0 2.1 convolution_bitcast_fusion.6
  281.1 2.4 copy.71
  283.4 2.3 copy.72
  287.9 19.2 %all-gather.3 = f32[8,1,8192]{2,1,0:T(1,128)S(1)} all-gather(f32[1,1,8192]{2,1,0:T(1,128)S(1)} %bitcast.171), channel_id=1, replica_groups=mesh['clu'=32,'sub'=8] {'sub'}, dimensions={0}, use_global_device_ids=true | all-gather | bytes 294912 | tf_op jit(solution)/shard_map/all_gather | solution.py:60
  308.3 3.1 fusion.53
  312.6 2.5 copy.74
  315.1 1.8 convolution_bitcast_fusion.5
  317.1 7.0 %collective-permute-start.16 = (f32[128,3,128]{2,1,0:T(4,128)S(1)}, f32[128,3,128]{2,1,0:T(4,128)S(1)}, u32[]{:S(2)}, u32[]{:S(2)}) collective-permute-start(f32[128,3,128]{2,1,0:T(4,128)S(1)} %get-tuple-element.22), channel_id=1, source_target_pairs={{0,8},{8,0},{16,24},{24,16},{32,40},{40,32},{48,56},{56,48},{64,72... | collective-permute-start | bytes 589832 | tf_op jit(solution)/shard_map/ppermute | solution.py:16
  327.0 4.9 collective-permute-done.19
  334.0 3.4 collective-permute-done.17
  338.1 2.1 convolution_bitcast_fusion.4
  340.2 2.4 copy.76
  342.6 2.3 copy.77
  347.0 18.4 %all-gather.4 = f32[8,1,8192]{2,1,0:T(1,128)S(1)} all-gather(f32[1,1,8192]{2,1,0:T(1,128)S(1)} %bitcast.172), channel_id=1, replica_groups=mesh['clu'=32,'sub'=8] {'sub'}, dimensions={0}, use_global_device_ids=true | all-gather | bytes 294912 | tf_op jit(solution)/shard_map/all_gather | solution.py:60
  368.5 80.5 %all-reduce.1 = (f32[128]{0:T(128)S(1)}, f32[128]{0:T(128)S(1)}) all-reduce(f32[128]{0:T(128)S(1)} %get-tuple-element.5, f32[128]{0:T(128)S(1)} %get-tuple-element.4), channel_id=1, replica_groups=mesh['clu'=32,'sub'=8] {'clu','sub'}, use_global_device_ids=true, to_apply=%region_5.0 | all-reduce | flops 256 | bytes 2048 | tf_op jit(solution)/shard_map/psum | solution.py:76
  450.3 3.1 fusion.51
  454.6 2.5 copy.79
  457.1 1.8 convolution_bitcast_fusion.3
  463.0 4.9 collective-permute-done.23
  471.0 2.7 collective-permute-done.21
  474.5 2.1 convolution_bitcast_fusion.2
  476.6 2.4 copy.81
  479.0 2.3 copy.82
  483.4 19.4 %all-gather.5 = f32[8,1,8192]{2,1,0:T(1,128)S(1)} all-gather(f32[1,1,8192]{2,1,0:T(1,128)S(1)} %bitcast.173), channel_id=1, replica_groups=mesh['clu'=32,'sub'=8] {'sub'}, dimensions={0}, use_global_device_ids=true | all-gather | bytes 294912 | tf_op jit(solution)/shard_map/all_gather | solution.py:60
  505.8 3.1 fusion.49
  510.1 2.5 copy.84
  514.7 7.0 %collective-permute-start.24 = (f32[128,3,128]{2,1,0:T(4,128)S(1)}, f32[128,3,128]{2,1,0:T(4,128)S(1)}, u32[]{:S(2)}, u32[]{:S(2)}) collective-permute-start(f32[128,3,128]{2,1,0:T(4,128)S(1)} %get-tuple-element.14), channel_id=1, source_target_pairs={{0,8},{8,0},{16,24},{24,16},{32,40},{40,32},{48,56},{56,48},{64,72... | collective-permute-start | bytes 589832 | tf_op jit(solution)/shard_map/ppermute | solution.py:16
  525.5 4.0 collective-permute-done.27
  531.5 5.0 collective-permute-done.25
  537.3 2.1 convolution_bitcast_fusion
  539.4 2.4 copy.86
  541.7 2.3 copy.87
  546.2 18.4 %all-gather.6 = f32[8,1,8192]{2,1,0:T(1,128)S(1)} all-gather(f32[1,1,8192]{2,1,0:T(1,128)S(1)} %bitcast.174), channel_id=1, replica_groups=mesh['clu'=32,'sub'=8] {'sub'}, dimensions={0}, use_global_device_ids=true | all-gather | bytes 294912 | tf_op jit(solution)/shard_map/all_gather | solution.py:60
  567.7 78.6 %all-reduce = (f32[128]{0:T(128)}, f32[128]{0:T(128)}) all-reduce(f32[128]{0:T(128)S(1)} %get-tuple-element.3, f32[128]{0:T(128)S(1)} %get-tuple-element.2), channel_id=1, replica_groups=mesh['clu'=32,'sub'=8] {'clu','sub'}, use_global_device_ids=true, to_apply=%region_9.0 | all-reduce | flops 256 | bytes 2048 | tf_op jit(solution)/shard_map/psum | solution.py:76
  647.0 2.9 multiply_subtract_fusion
  (139 shorter events, 99.4 us)
Async XLA Ops:
  0.6 27.7 %copy-start = (f32[64,1536]{1,0:T(8,128)S(1)}, f32[64,1536]{1,0:T(8,128)}, u32[]{:S(2)}) copy-start(f32[64,1536]{1,0:T(8,128)} %param.13) | copy-start | bytes 1179652
  0.6 4.2 copy-start.4
  4.1 8.2 %copy-start.5 = (s32[8]{0:T(128)S(1)}, s32[8]{0:T(128)}, u32[]{:S(2)}) copy-start(s32[8]{0:T(128)} %param.17) | copy-start | bytes 100
  4.1 9.4 %copy-start.6 = (s32[1,4]{1,0:T(1,128)S(1)}, s32[1,4]{1,0:T(1,128)}, u32[]{:S(2)}) copy-start(s32[1,4]{1,0:T(1,128)} %param.16) | copy-start | bytes 52
  5.7 8.6 %collective-permute-start = (f32[128,3,128]{2,1,0:T(4,128)S(1)}, f32[128,3,128]{2,1,0:T(4,128)S(1)}, u32[]{:S(2)}, u32[]{:S(2)}) collective-permute-start(f32[128,3,128]{2,1,0:T(4,128)S(1)} %get-tuple-element.38), channel_id=1, source_target_pairs={{0,8},{8,0},{16,24},{24,16},{32,40},{40,32},{48,56},{56,48},{64,72... | collective-permute-start | bytes 589832 | tf_op jit(solution)/shard_map/ppermute | solution.py:16
  9.0 7.8 %collective-permute-start.3 = (f32[128,3,128]{2,1,0:T(4,128)S(1)}, f32[128,3,128]{2,1,0:T(4,128)S(1)}, u32[]{:S(2)}, u32[]{:S(2)}) collective-permute-start(f32[128,3,128]{2,1,0:T(4,128)S(1)} %get-tuple-element.39), channel_id=1, source_target_pairs={{0,1},{1,0},{2,3},{3,2},{4,5},{5,4},{6,7},{7,6},{8,9},{9,8},{10,11... | collective-permute-start | bytes 589832 | tf_op jit(solution)/shard_map/ppermute | solution.py:16
  9.0 9.1 %collective-permute-start.2 = (f32[128,3,128]{2,1,0:T(4,128)S(1)}, f32[128,3,128]{2,1,0:T(4,128)S(1)}, u32[]{:S(2)}, u32[]{:S(2)}) collective-permute-start(f32[128,3,128]{2,1,0:T(4,128)S(1)} %get-tuple-element.40), channel_id=1, source_target_pairs={{0,32},{8,40},{16,48},{24,56},{32,0},{40,8},{48,16},{56,24},{64,96... | collective-permute-start | bytes 589832 | tf_op jit(solution)/shard_map/ppermute | solution.py:16
  11.8 12.0 %collective-permute-start.1 = (f32[128,3,128]{2,1,0:T(4,128)S(1)}, f32[128,3,128]{2,1,0:T(4,128)S(1)}, u32[]{:S(2)}, u32[]{:S(2)}) collective-permute-start(f32[128,3,128]{2,1,0:T(4,128)S(1)} %get-tuple-element.41), channel_id=1, source_target_pairs={{0,16},{8,24},{16,0},{24,8},{32,48},{40,56},{48,32},{56,40},{64,80... | collective-permute-start | bytes 589832 | tf_op jit(solution)/shard_map/ppermute | solution.py:16
  18.1 34.3 %copy-start.3 = (f32[64,512]{1,0:T(8,128)S(1)}, f32[64,512]{1,0:T(8,128)}, u32[]{:S(2)}) copy-start(f32[64,512]{1,0:T(8,128)} %param.14) | copy-start | bytes 393220
  61.6 9.5 %collective-permute-start.4 = (f32[128,3,128]{2,1,0:T(4,128)S(1)}, f32[128,3,128]{2,1,0:T(4,128)S(1)}, u32[]{:S(2)}, u32[]{:S(2)}) collective-permute-start(f32[128,3,128]{2,1,0:T(4,128)S(1)} %get-tuple-element.34), channel_id=1, source_target_pairs={{0,8},{8,0},{16,24},{24,16},{32,40},{40,32},{48,56},{56,48},{64,72... | collective-permute-start | bytes 589832 | tf_op jit(solution)/shard_map/ppermute | solution.py:16
  68.6 7.8 %collective-permute-start.7 = (f32[128,3,128]{2,1,0:T(4,128)S(1)}, f32[128,3,128]{2,1,0:T(4,128)S(1)}, u32[]{:S(2)}, u32[]{:S(2)}) collective-permute-start(f32[128,3,128]{2,1,0:T(4,128)S(1)} %get-tuple-element.35), channel_id=1, source_target_pairs={{0,1},{1,0},{2,3},{3,2},{4,5},{5,4},{6,7},{7,6},{8,9},{9,8},{10,11... | collective-permute-start | bytes 589832 | tf_op jit(solution)/shard_map/ppermute | solution.py:16
  69.4 9.0 %collective-permute-start.6 = (f32[128,3,128]{2,1,0:T(4,128)S(1)}, f32[128,3,128]{2,1,0:T(4,128)S(1)}, u32[]{:S(2)}, u32[]{:S(2)}) collective-permute-start(f32[128,3,128]{2,1,0:T(4,128)S(1)} %get-tuple-element.36), channel_id=1, source_target_pairs={{0,32},{8,40},{16,48},{24,56},{32,0},{40,8},{48,16},{56,24},{64,96... | collective-permute-start | bytes 589832 | tf_op jit(solution)/shard_map/ppermute | solution.py:16
  71.0 11.4 %collective-permute-start.5 = (f32[128,3,128]{2,1,0:T(4,128)S(1)}, f32[128,3,128]{2,1,0:T(4,128)S(1)}, u32[]{:S(2)}, u32[]{:S(2)}) collective-permute-start(f32[128,3,128]{2,1,0:T(4,128)S(1)} %get-tuple-element.37), channel_id=1, source_target_pairs={{0,16},{8,24},{16,0},{24,8},{32,48},{40,56},{48,32},{56,40},{64,80... | collective-permute-start | bytes 589832 | tf_op jit(solution)/shard_map/ppermute | solution.py:16
  119.2 10.4 %collective-permute-start.8 = (f32[128,3,128]{2,1,0:T(4,128)S(1)}, f32[128,3,128]{2,1,0:T(4,128)S(1)}, u32[]{:S(2)}, u32[]{:S(2)}) collective-permute-start(f32[128,3,128]{2,1,0:T(4,128)S(1)} %get-tuple-element.30), channel_id=1, source_target_pairs={{0,8},{8,0},{16,24},{24,16},{32,40},{40,32},{48,56},{56,48},{64,72... | collective-permute-start | bytes 589832 | tf_op jit(solution)/shard_map/ppermute | solution.py:16
  126.1 7.8 %collective-permute-start.11 = (f32[128,3,128]{2,1,0:T(4,128)S(1)}, f32[128,3,128]{2,1,0:T(4,128)S(1)}, u32[]{:S(2)}, u32[]{:S(2)}) collective-permute-start(f32[128,3,128]{2,1,0:T(4,128)S(1)} %get-tuple-element.31), channel_id=1, source_target_pairs={{0,1},{1,0},{2,3},{3,2},{4,5},{5,4},{6,7},{7,6},{8,9},{9,8},{10,11... | collective-permute-start | bytes 589832 | tf_op jit(solution)/shard_map/ppermute | solution.py:16
  126.1 9.8 %collective-permute-start.10 = (f32[128,3,128]{2,1,0:T(4,128)S(1)}, f32[128,3,128]{2,1,0:T(4,128)S(1)}, u32[]{:S(2)}, u32[]{:S(2)}) collective-permute-start(f32[128,3,128]{2,1,0:T(4,128)S(1)} %get-tuple-element.32), channel_id=1, source_target_pairs={{0,32},{8,40},{16,48},{24,56},{32,0},{40,8},{48,16},{56,24},{64,96... | collective-permute-start | bytes 589832 | tf_op jit(solution)/shard_map/ppermute | solution.py:16
  129.5 10.9 %collective-permute-start.9 = (f32[128,3,128]{2,1,0:T(4,128)S(1)}, f32[128,3,128]{2,1,0:T(4,128)S(1)}, u32[]{:S(2)}, u32[]{:S(2)}) collective-permute-start(f32[128,3,128]{2,1,0:T(4,128)S(1)} %get-tuple-element.33), channel_id=1, source_target_pairs={{0,16},{8,24},{16,0},{24,8},{32,48},{40,56},{48,32},{56,40},{64,80... | collective-permute-start | bytes 589832 | tf_op jit(solution)/shard_map/ppermute | solution.py:16
  262.2 4.4 collective-permute-start.12
  263.0 7.8 %collective-permute-start.15 = (f32[128,3,128]{2,1,0:T(4,128)S(1)}, f32[128,3,128]{2,1,0:T(4,128)S(1)}, u32[]{:S(2)}, u32[]{:S(2)}) collective-permute-start(f32[128,3,128]{2,1,0:T(4,128)S(1)} %get-tuple-element.27), channel_id=1, source_target_pairs={{0,1},{1,0},{2,3},{3,2},{4,5},{5,4},{6,7},{7,6},{8,9},{9,8},{10,11... | collective-permute-start | bytes 589832 | tf_op jit(solution)/shard_map/ppermute | solution.py:16
  264.2 9.0 %collective-permute-start.14 = (f32[128,3,128]{2,1,0:T(4,128)S(1)}, f32[128,3,128]{2,1,0:T(4,128)S(1)}, u32[]{:S(2)}, u32[]{:S(2)}) collective-permute-start(f32[128,3,128]{2,1,0:T(4,128)S(1)} %get-tuple-element.28), channel_id=1, source_target_pairs={{0,32},{8,40},{16,48},{24,56},{32,0},{40,8},{48,16},{56,24},{64,96... | collective-permute-start | bytes 589832 | tf_op jit(solution)/shard_map/ppermute | solution.py:16
  265.3 12.9 %collective-permute-start.13 = (f32[128,3,128]{2,1,0:T(4,128)S(1)}, f32[128,3,128]{2,1,0:T(4,128)S(1)}, u32[]{:S(2)}, u32[]{:S(2)}) collective-permute-start(f32[128,3,128]{2,1,0:T(4,128)S(1)} %get-tuple-element.29), channel_id=1, source_target_pairs={{0,16},{8,24},{16,0},{24,8},{32,48},{40,56},{48,32},{56,40},{64,80... | collective-permute-start | bytes 589832 | tf_op jit(solution)/shard_map/ppermute | solution.py:16
  317.1 9.1 %collective-permute-start.16 = (f32[128,3,128]{2,1,0:T(4,128)S(1)}, f32[128,3,128]{2,1,0:T(4,128)S(1)}, u32[]{:S(2)}, u32[]{:S(2)}) collective-permute-start(f32[128,3,128]{2,1,0:T(4,128)S(1)} %get-tuple-element.22), channel_id=1, source_target_pairs={{0,8},{8,0},{16,24},{24,16},{32,40},{40,32},{48,56},{56,48},{64,72... | collective-permute-start | bytes 589832 | tf_op jit(solution)/shard_map/ppermute | solution.py:16
  324.1 7.8 %collective-permute-start.19 = (f32[128,3,128]{2,1,0:T(4,128)S(1)}, f32[128,3,128]{2,1,0:T(4,128)S(1)}, u32[]{:S(2)}, u32[]{:S(2)}) collective-permute-start(f32[128,3,128]{2,1,0:T(4,128)S(1)} %get-tuple-element.23), channel_id=1, source_target_pairs={{0,1},{1,0},{2,3},{3,2},{4,5},{5,4},{6,7},{7,6},{8,9},{9,8},{10,11... | collective-permute-start | bytes 589832 | tf_op jit(solution)/shard_map/ppermute | solution.py:16
  324.1 9.2 %collective-permute-start.18 = (f32[128,3,128]{2,1,0:T(4,128)S(1)}, f32[128,3,128]{2,1,0:T(4,128)S(1)}, u32[]{:S(2)}, u32[]{:S(2)}) collective-permute-start(f32[128,3,128]{2,1,0:T(4,128)S(1)} %get-tuple-element.24), channel_id=1, source_target_pairs={{0,32},{8,40},{16,48},{24,56},{32,0},{40,8},{48,16},{56,24},{64,96... | collective-permute-start | bytes 589832 | tf_op jit(solution)/shard_map/ppermute | solution.py:16
  325.9 11.6 %collective-permute-start.17 = (f32[128,3,128]{2,1,0:T(4,128)S(1)}, f32[128,3,128]{2,1,0:T(4,128)S(1)}, u32[]{:S(2)}, u32[]{:S(2)}) collective-permute-start(f32[128,3,128]{2,1,0:T(4,128)S(1)} %get-tuple-element.25), channel_id=1, source_target_pairs={{0,16},{8,24},{16,0},{24,8},{32,48},{40,56},{48,32},{56,40},{64,80... | collective-permute-start | bytes 589832 | tf_op jit(solution)/shard_map/ppermute | solution.py:16
  459.1 3.1 collective-permute-start.20
  460.1 7.8 %collective-permute-start.23 = (f32[128,3,128]{2,1,0:T(4,128)S(1)}, f32[128,3,128]{2,1,0:T(4,128)S(1)}, u32[]{:S(2)}, u32[]{:S(2)}) collective-permute-start(f32[128,3,128]{2,1,0:T(4,128)S(1)} %get-tuple-element.19), channel_id=1, source_target_pairs={{0,1},{1,0},{2,3},{3,2},{4,5},{5,4},{6,7},{7,6},{8,9},{9,8},{10,11... | collective-permute-start | bytes 589832 | tf_op jit(solution)/shard_map/ppermute | solution.py:16
  461.4 9.0 %collective-permute-start.22 = (f32[128,3,128]{2,1,0:T(4,128)S(1)}, f32[128,3,128]{2,1,0:T(4,128)S(1)}, u32[]{:S(2)}, u32[]{:S(2)}) collective-permute-start(f32[128,3,128]{2,1,0:T(4,128)S(1)} %get-tuple-element.20), channel_id=1, source_target_pairs={{0,32},{8,40},{16,48},{24,56},{32,0},{40,8},{48,16},{56,24},{64,96... | collective-permute-start | bytes 589832 | tf_op jit(solution)/shard_map/ppermute | solution.py:16
  462.3 11.5 %collective-permute-start.21 = (f32[128,3,128]{2,1,0:T(4,128)S(1)}, f32[128,3,128]{2,1,0:T(4,128)S(1)}, u32[]{:S(2)}, u32[]{:S(2)}) collective-permute-start(f32[128,3,128]{2,1,0:T(4,128)S(1)} %get-tuple-element.21), channel_id=1, source_target_pairs={{0,16},{8,24},{16,0},{24,8},{32,48},{40,56},{48,32},{56,40},{64,80... | collective-permute-start | bytes 589832 | tf_op jit(solution)/shard_map/ppermute | solution.py:16
  504.9 0.9 copy-start.1
  514.7 10.0 %collective-permute-start.24 = (f32[128,3,128]{2,1,0:T(4,128)S(1)}, f32[128,3,128]{2,1,0:T(4,128)S(1)}, u32[]{:S(2)}, u32[]{:S(2)}) collective-permute-start(f32[128,3,128]{2,1,0:T(4,128)S(1)} %get-tuple-element.14), channel_id=1, source_target_pairs={{0,8},{8,0},{16,24},{24,16},{32,40},{40,32},{48,56},{56,48},{64,72... | collective-permute-start | bytes 589832 | tf_op jit(solution)/shard_map/ppermute | solution.py:16
  521.7 7.8 %collective-permute-start.27 = (f32[128,3,128]{2,1,0:T(4,128)S(1)}, f32[128,3,128]{2,1,0:T(4,128)S(1)}, u32[]{:S(2)}, u32[]{:S(2)}) collective-permute-start(f32[128,3,128]{2,1,0:T(4,128)S(1)} %get-tuple-element.15), channel_id=1, source_target_pairs={{0,1},{1,0},{2,3},{3,2},{4,5},{5,4},{6,7},{7,6},{8,9},{9,8},{10,11... | collective-permute-start | bytes 589832 | tf_op jit(solution)/shard_map/ppermute | solution.py:16
  521.7 9.2 %collective-permute-start.26 = (f32[128,3,128]{2,1,0:T(4,128)S(1)}, f32[128,3,128]{2,1,0:T(4,128)S(1)}, u32[]{:S(2)}, u32[]{:S(2)}) collective-permute-start(f32[128,3,128]{2,1,0:T(4,128)S(1)} %get-tuple-element.16), channel_id=1, source_target_pairs={{0,32},{8,40},{16,48},{24,56},{32,0},{40,8},{48,16},{56,24},{64,96... | collective-permute-start | bytes 589832 | tf_op jit(solution)/shard_map/ppermute | solution.py:16
  523.4 13.2 %collective-permute-start.25 = (f32[128,3,128]{2,1,0:T(4,128)S(1)}, f32[128,3,128]{2,1,0:T(4,128)S(1)}, u32[]{:S(2)}, u32[]{:S(2)}) collective-permute-start(f32[128,3,128]{2,1,0:T(4,128)S(1)} %get-tuple-element.17), channel_id=1, source_target_pairs={{0,16},{8,24},{16,0},{24,8},{32,48},{40,56},{48,32},{56,40},{64,80... | collective-permute-start | bytes 589832 | tf_op jit(solution)/shard_map/ppermute | solution.py:16
  545.3 101.8 %copy-start.2 = (f32[128,1536]{1,0:T(8,128)S(1)}, f32[128,1536]{1,0:T(8,128)}, u32[]{:S(2)}) copy-start(f32[128,1536]{1,0:T(8,128)} %copy-done.1) | copy-start | bytes 2359300
where the time goes:
time: 661 us; the launch traced here: 650 us
  blocking collectives  375 us (57%)
  matrix products  70.3 us (11%)
  waiting for transfers between devices  63.1 us (10%)
  starting transfers between devices  53 us (8%)
  local copies, waits for them, and re-layouts  52.9 us (8%)
  other arithmetic  33.6 us (5%)
    psum x3, blocking collectives, on_device(): cross_all, image_all = lax.psum((cross_sum, image_sum), ('clu', 'sub'))  240 us
    all_gather x7, blocking collectives, coarse(): piece = lax.all_gather(flat, 'sub', axis=0, tiled=True)  135 us
    ppermute x28, waiting for transfers between devices, from_partner(): return lax.ppermute(value, axis, pairs)  63.1 us
    ppermute x28, starting transfers between devices, from_partner(): return lax.ppermute(value, axis, pairs)  53 us
    dot_general x7, matrix products, apply_local(): jnp.dot(vector.astype(jnp.bfloat16), matrix, preferred_element_type=jnp.f...  22.2 us
    mul x21, other arithmetic, assemble(): received.append(incoming * edge_gates[colour])  14.8 us
    transpose x7, local copies, waits for them, and re-layouts, assemble(): added = jnp.einsum('jq,kjb->kqb', onehot, joined, precision=HIGH)  14.7 us
    reshape x7, local copies, waits for them, and re-layouts, assemble(): blocked = product.reshape(cases, blocks, BLK)  14.5 us
  transfers between devices with their start and end apart: 28, of which 21 were waited for; matrix products, arithmetic and copies ran while one was open for 3% of the time, Pallas kernels for 0%

commit v1 on v0

--- a/solution.py
+++ b/solution.py
@@ -57,7 +57,9 @@
     def coarse(vector):
         coeffs = jnp.einsum("em,km->ek", rigid_modes, vector, precision=HIGH)
         flat = coeffs.reshape(1, E * cases)
-        piece = lax.all_gather(flat, "sub", axis=0, tiled=True)
+        piece = jnp.concatenate(
+            lax.all_to_all(jnp.stack([flat] * lax.axis_size("sub")), "sub", 0, 0), axis=0
+        )
         count = piece.shape[0]
         masked = (piece.reshape(count, E, cases) * same_group[:, None, None]).reshape(
             count * E, cases

time: 661 us -> 597 us (0.903)
  blocking collectives: 375 us -> 309 us
  waiting for transfers between devices: 63.1 us -> 73.4 us
  starting transfers between devices: 53 us -> 44.3 us
    all_gather x7 -> x0, blocking collectives: 135 us -> none  [coarse(): piece = lax.all_gather(flat, 'sub', axis=0, tiled=True)]
    all_to_all x0 -> x6, blocking collectives: none -> 75.9 us  [coarse(): lax.all_to_all(jnp.stack([flat] * lax.axis_size('sub')), 'sub', 0, 0)]
    ppermute x28, starting transfers between devices: 53 us -> 37 us  [from_partner(): return lax.ppermute(value, axis, pairs)]
    all_to_all x0 -> x1, waiting for transfers between devices: none -> 8.79 us  [coarse(): lax.all_to_all(jnp.stack([flat] * lax.axis_size('sub')), 'sub', 0, 0)]
    psum x3, blocking collectives: 240 us -> 233 us  [on_device(): cross_all, image_all = lax.psum((cross_sum, image_sum), ('clu', 'sub'))]
    all_to_all x0 -> x1, starting transfers between devices: none -> 7.29 us  [coarse(): lax.all_to_all(jnp.stack([flat] * lax.axis_size('sub')), 'sub', 0, 0)]
  transfers between devices with their start and end apart: 28 -> 29, of which waited for: 21 -> 22; matrix products, arithmetic and copies ran while one was open for 3% -> 3% of each run, Pallas kernels for 0% -> 0%
where the time goes in v1:
time: 597 us; the launch traced here: 586 us
  blocking collectives  309 us (52%)
  waiting for transfers between devices  73.4 us (12%)
  matrix products  70.4 us (12%)
  local copies, waits for them, and re-layouts  54.6 us (9%)
  starting transfers between devices  44.3 us (7%)
  other arithmetic  33 us (6%)
    psum x3, blocking collectives, on_device(): cross_all, image_all = lax.psum((cross_sum, image_sum), ('clu', 'sub'))  233 us
    all_to_all x6, blocking collectives, coarse(): lax.all_to_all(jnp.stack([flat] * lax.axis_size('sub')), 'sub', 0, 0)  75.9 us
    ppermute x28, waiting for transfers between devices, from_partner(): return lax.ppermute(value, axis, pairs)  64.6 us
    ppermute x28, starting transfers between devices, from_partner(): return lax.ppermute(value, axis, pairs)  37 us
    dot_general x7, matrix products, apply_local(): jnp.dot(vector.astype(jnp.bfloat16), matrix, preferred_element_type=jnp.f...  22.2 us
    transpose x7, local copies, waits for them, and re-layouts, assemble(): added = jnp.einsum('jq,kjb->kqb', onehot, joined, precision=HIGH)  14.7 us
    reshape x7, local copies, waits for them, and re-layouts, assemble(): blocked = product.reshape(cases, blocks, BLK)  14.6 us
    reshape x7, local copies, waits for them, and re-layouts, assemble(): return product + added.reshape(cases, blocks * BLK)  13.9 us
  transfers between devices with their start and end apart: 29, of which 22 were waited for; matrix products, arithmetic and copies ran while one was open for 3% of the time, Pallas kernels for 0%

profile of v1, /device:TPU:1, one launch (start us, length us, event | category | flops | bytes accessed | tf_op | source)
XLA Modules:
  0.0 586.2 jit_solution(4157610508370626822)
XLA Ops:
  0.7 3.4 fusion.61
  5.7 3.3 collective-permute-start
  9.0 2.8 collective-permute-start.2
  13.6 3.2 collective-permute-done.3
  18.8 5.1 collective-permute-done.1
  28.2 2.1 convolution_bitcast_fusion.20
  31.1 7.3 %all-to-all-start = ((f32[8,1,8192]{2,1,0:T(1,128)}), f32[8,1,8192]{2,1,0:T(1,128)S(1)}, u32[]{:S(2)}, u32[]{:S(2)}) async-start(f32[8,1,8192]{2,1,0:T(1,128)} %stack.21), calls=%async_computation | async-start | bytes 524288 | tf_op jit(solution)/shard_map/all_to_all | solution.py:61
  39.8 8.8 %all-to-all-done = f32[8,1,8192]{2,1,0:T(1,128)S(1)} async-done(((f32[8,1,8192]{2,1,0:T(1,128)}), f32[8,1,8192]{2,1,0:T(1,128)S(1)}, u32[]{:S(2)}, u32[]{:S(2)}) %all-to-all-start) | async-done | bytes 262176 | tf_op jit(solution)/shard_map/all_to_all | solution.py:61
  49.0 2.1 convolution_subtract_fusion.6
  51.1 3.1 fusion.59
  57.9 2.7 collective-permute-start.4
  63.4 5.0 collective-permute-done.7
  70.6 3.3 collective-permute-done.5
  74.5 2.1 convolution_bitcast_fusion.10
  81.6 12.7 %all_to_all.35 = f32[8,1,8192]{2,1,0:T(1,128)S(1)} all-to-all(f32[8,1,8192]{2,1,0:T(1,128)S(1)} %stack.22), channel_id=1, replica_groups=mesh['clu'=32,'sub'=8] {'sub'}, dimensions={0} | all-to-all | bytes 524288 | tf_op jit(solution)/shard_map/all_to_all | solution.py:61
  95.5 3.1 fusion.57
  99.8 2.5 copy.99
  104.3 2.6 collective-permute-start.8
  107.2 3.3 collective-permute-start.10
  111.2 3.5 collective-permute-done.11
  117.6 3.9 collective-permute-done.9
  122.0 2.1 convolution_bitcast_fusion.8
  124.1 2.4 copy.101
  126.5 2.3 copy.102
  131.1 12.6 %all_to_all.36 = f32[8,1,8192]{2,1,0:T(1,128)S(1)} all-to-all(f32[8,1,8192]{2,1,0:T(1,128)S(1)} %stack.23), channel_id=1, replica_groups=mesh['clu'=32,'sub'=8] {'sub'}, dimensions={0} | all-to-all | bytes 524288 | tf_op jit(solution)/shard_map/all_to_all | solution.py:61
  145.8 84.5 %all-reduce.2 = (f32[128]{0:T(128)S(1)}, f32[128]{0:T(128)S(1)}) all-reduce(f32[128]{0:T(128)S(1)} %get-tuple-element.7, f32[128]{0:T(128)S(1)} %get-tuple-element.6), channel_id=1, replica_groups=mesh['clu'=32,'sub'=8] {'clu','sub'}, use_global_device_ids=true, to_apply=%region_1.0 | all-reduce | flops 256 | bytes 2048 | tf_op jit(solution)/shard_map/psum | solution.py:78
  231.6 3.1 fusion.55
  235.8 2.5 copy.104
  246.1 3.4 collective-permute-done.15
  252.7 4.4 collective-permute-done.13
  257.7 2.1 convolution_bitcast_fusion.6
  259.8 2.4 copy.106
  262.1 2.3 copy.107
  266.7 12.6 %all_to_all.37 = f32[8,1,8192]{2,1,0:T(1,128)S(1)} all-to-all(f32[8,1,8192]{2,1,0:T(1,128)S(1)} %stack.24), channel_id=1, replica_groups=mesh['clu'=32,'sub'=8] {'sub'}, dimensions={0} | all-to-all | bytes 524288 | tf_op jit(solution)/shard_map/all_to_all | solution.py:61
  280.5 3.1 fusion.53
  284.8 2.5 copy.109
  289.4 2.8 collective-permute-start.16
  292.4 1.9 collective-permute-start.18
  295.0 4.9 collective-permute-done.19
  302.3 3.6 collective-permute-done.17
  306.5 2.1 convolution_bitcast_fusion.4
  308.6 2.4 copy.111
  311.0 2.3 copy.112
  315.6 12.6 %all_to_all.38 = f32[8,1,8192]{2,1,0:T(1,128)S(1)} all-to-all(f32[8,1,8192]{2,1,0:T(1,128)S(1)} %stack.25), channel_id=1, replica_groups=mesh['clu'=32,'sub'=8] {'sub'}, dimensions={0} | all-to-all | bytes 524288 | tf_op jit(solution)/shard_map/all_to_all | solution.py:61
  331.2 75.0 %all-reduce.1 = (f32[128]{0:T(128)S(1)}, f32[128]{0:T(128)S(1)}) all-reduce(f32[128]{0:T(128)S(1)} %get-tuple-element.5, f32[128]{0:T(128)S(1)} %get-tuple-element.4), channel_id=1, replica_groups=mesh['clu'=32,'sub'=8] {'clu','sub'}, use_global_device_ids=true, to_apply=%region_5.0 | all-reduce | flops 256 | bytes 2048 | tf_op jit(solution)/shard_map/psum | solution.py:78
  407.5 3.1 fusion.51
  411.7 2.5 copy.114
  420.7 4.9 collective-permute-done.23
  428.7 2.9 collective-permute-done.21
  432.3 2.1 convolution_bitcast_fusion.2
  434.4 2.4 copy.116
  436.8 2.3 copy.117
  441.3 12.9 %all_to_all.39 = f32[8,1,8192]{2,1,0:T(1,128)S(1)} all-to-all(f32[8,1,8192]{2,1,0:T(1,128)S(1)} %stack.26), channel_id=1, replica_groups=mesh['clu'=32,'sub'=8] {'sub'}, dimensions={0} | all-to-all | bytes 524288 | tf_op jit(solution)/shard_map/all_to_all | solution.py:61
  457.2 3.1 fusion.49
  461.5 2.5 copy.119
  466.1 2.7 collective-permute-start.24
  472.6 4.0 collective-permute-done.27
  478.8 4.7 collective-permute-done.25
  484.1 2.1 convolution_bitcast_fusion
  486.2 2.4 copy.121
  488.6 2.3 copy.122
  493.2 12.6 %all_to_all.40 = f32[8,1,8192]{2,1,0:T(1,128)S(1)} all-to-all(f32[8,1,8192]{2,1,0:T(1,128)S(1)} %stack.27), channel_id=1, replica_groups=mesh['clu'=32,'sub'=8] {'sub'}, dimensions={0} | all-to-all | bytes 524288 | tf_op jit(solution)/shard_map/all_to_all | solution.py:61
  508.8 73.3 %all-reduce = (f32[128]{0:T(128)}, f32[128]{0:T(128)}) all-reduce(f32[128]{0:T(128)S(1)} %get-tuple-element.3, f32[128]{0:T(128)S(1)} %get-tuple-element.2), channel_id=1, replica_groups=mesh['clu'=32,'sub'=8] {'clu','sub'}, use_global_device_ids=true, to_apply=%region_9.0 | all-reduce | flops 256 | bytes 2048 | tf_op jit(solution)/shard_map/psum | solution.py:78
  582.9 2.9 multiply_subtract_fusion
  (147 shorter events, 103.1 us)
Async XLA Ops:
  0.6 27.6 %copy-start = (f32[64,1536]{1,0:T(8,128)S(1)}, f32[64,1536]{1,0:T(8,128)}, u32[]{:S(2)}) copy-start(f32[64,1536]{1,0:T(8,128)} %param.13) | copy-start | bytes 1179652
  0.6 4.2 copy-start.4
  4.1 8.1 %copy-start.5 = (s32[1,4]{1,0:T(1,128)S(1)}, s32[1,4]{1,0:T(1,128)}, u32[]{:S(2)}) copy-start(s32[1,4]{1,0:T(1,128)} %param.16) | copy-start | bytes 52
  5.7 7.2 %collective-permute-start = (f32[128,3,128]{2,1,0:T(4,128)S(1)}, f32[128,3,128]{2,1,0:T(4,128)S(1)}, u32[]{:S(2)}, u32[]{:S(2)}) collective-permute-start(f32[128,3,128]{2,1,0:T(4,128)S(1)} %get-tuple-element.38), channel_id=1, source_target_pairs={{0,8},{8,0},{16,24},{24,16},{32,40},{40,32},{48,56},{56,48},{64,72... | collective-permute-start | bytes 589832 | tf_op jit(solution)/shard_map/ppermute | solution.py:16
  9.0 7.8 %collective-permute-start.3 = (f32[128,3,128]{2,1,0:T(4,128)S(1)}, f32[128,3,128]{2,1,0:T(4,128)S(1)}, u32[]{:S(2)}, u32[]{:S(2)}) collective-permute-start(f32[128,3,128]{2,1,0:T(4,128)S(1)} %get-tuple-element.39), channel_id=1, source_target_pairs={{0,1},{1,0},{2,3},{3,2},{4,5},{5,4},{6,7},{7,6},{8,9},{9,8},{10,11... | collective-permute-start | bytes 589832 | tf_op jit(solution)/shard_map/ppermute | solution.py:16
  9.0 9.1 %collective-permute-start.2 = (f32[128,3,128]{2,1,0:T(4,128)S(1)}, f32[128,3,128]{2,1,0:T(4,128)S(1)}, u32[]{:S(2)}, u32[]{:S(2)}) collective-permute-start(f32[128,3,128]{2,1,0:T(4,128)S(1)} %get-tuple-element.40), channel_id=1, source_target_pairs={{0,32},{8,40},{16,48},{24,56},{32,0},{40,8},{48,16},{56,24},{64,96... | collective-permute-start | bytes 589832 | tf_op jit(solution)/shard_map/ppermute | solution.py:16
  11.8 12.0 %collective-permute-start.1 = (f32[128,3,128]{2,1,0:T(4,128)S(1)}, f32[128,3,128]{2,1,0:T(4,128)S(1)}, u32[]{:S(2)}, u32[]{:S(2)}) collective-permute-start(f32[128,3,128]{2,1,0:T(4,128)S(1)} %get-tuple-element.41), channel_id=1, source_target_pairs={{0,16},{8,24},{16,0},{24,8},{32,48},{40,56},{48,32},{56,40},{64,80... | collective-permute-start | bytes 589832 | tf_op jit(solution)/shard_map/ppermute | solution.py:16
  23.9 14.6 %copy-start.6 = (s32[8]{0:T(128)S(1)}, s32[8]{0:T(128)}, u32[]{:S(2)}) copy-start(s32[8]{0:T(128)} %param.17) | copy-start | bytes 100
  23.9 24.8 %copy-start.3 = (f32[64,512]{1,0:T(8,128)S(1)}, f32[64,512]{1,0:T(8,128)}, u32[]{:S(2)}) copy-start(f32[64,512]{1,0:T(8,128)} %param.14) | copy-start | bytes 393220
  31.1 17.5 %all-to-all-start = ((f32[8,1,8192]{2,1,0:T(1,128)}), f32[8,1,8192]{2,1,0:T(1,128)S(1)}, u32[]{:S(2)}, u32[]{:S(2)}) async-start(f32[8,1,8192]{2,1,0:T(1,128)} %stack.21), calls=%async_computation | async-start | bytes 524288 | tf_op jit(solution)/shard_map/all_to_all | solution.py:61
  57.9 4.8 collective-permute-start.4
  60.6 7.8 %collective-permute-start.7 = (f32[128,3,128]{2,1,0:T(4,128)S(1)}, f32[128,3,128]{2,1,0:T(4,128)S(1)}, u32[]{:S(2)}, u32[]{:S(2)}) collective-permute-start(f32[128,3,128]{2,1,0:T(4,128)S(1)} %get-tuple-element.35), channel_id=1, source_target_pairs={{0,1},{1,0},{2,3},{3,2},{4,5},{5,4},{6,7},{7,6},{8,9},{9,8},{10,11... | collective-permute-start | bytes 589832 | tf_op jit(solution)/shard_map/ppermute | solution.py:16
  60.9 9.0 %collective-permute-start.6 = (f32[128,3,128]{2,1,0:T(4,128)S(1)}, f32[128,3,128]{2,1,0:T(4,128)S(1)}, u32[]{:S(2)}, u32[]{:S(2)}) collective-permute-start(f32[128,3,128]{2,1,0:T(4,128)S(1)} %get-tuple-element.36), channel_id=1, source_target_pairs={{0,32},{8,40},{16,48},{24,56},{32,0},{40,8},{48,16},{56,24},{64,96... | collective-permute-start | bytes 589832 | tf_op jit(solution)/shard_map/ppermute | solution.py:16
  62.5 11.4 %collective-permute-start.5 = (f32[128,3,128]{2,1,0:T(4,128)S(1)}, f32[128,3,128]{2,1,0:T(4,128)S(1)}, u32[]{:S(2)}, u32[]{:S(2)}) collective-permute-start(f32[128,3,128]{2,1,0:T(4,128)S(1)} %get-tuple-element.37), channel_id=1, source_target_pairs={{0,16},{8,24},{16,0},{24,8},{32,48},{40,56},{48,32},{56,40},{64,80... | collective-permute-start | bytes 589832 | tf_op jit(solution)/shard_map/ppermute | solution.py:16
  104.3 6.2 %collective-permute-start.8 = (f32[128,3,128]{2,1,0:T(4,128)S(1)}, f32[128,3,128]{2,1,0:T(4,128)S(1)}, u32[]{:S(2)}, u32[]{:S(2)}) collective-permute-start(f32[128,3,128]{2,1,0:T(4,128)S(1)} %get-tuple-element.30), channel_id=1, source_target_pairs={{0,8},{8,0},{16,24},{24,16},{32,40},{40,32},{48,56},{56,48},{64,72... | collective-permute-start | bytes 589832 | tf_op jit(solution)/shard_map/ppermute | solution.py:16
  106.9 7.8 %collective-permute-start.11 = (f32[128,3,128]{2,1,0:T(4,128)S(1)}, f32[128,3,128]{2,1,0:T(4,128)S(1)}, u32[]{:S(2)}, u32[]{:S(2)}) collective-permute-start(f32[128,3,128]{2,1,0:T(4,128)S(1)} %get-tuple-element.31), channel_id=1, source_target_pairs={{0,1},{1,0},{2,3},{3,2},{4,5},{5,4},{6,7},{7,6},{8,9},{9,8},{10,11... | collective-permute-start | bytes 589832 | tf_op jit(solution)/shard_map/ppermute | solution.py:16
  107.2 9.6 %collective-permute-start.10 = (f32[128,3,128]{2,1,0:T(4,128)S(1)}, f32[128,3,128]{2,1,0:T(4,128)S(1)}, u32[]{:S(2)}, u32[]{:S(2)}) collective-permute-start(f32[128,3,128]{2,1,0:T(4,128)S(1)} %get-tuple-element.32), channel_id=1, source_target_pairs={{0,32},{8,40},{16,48},{24,56},{32,0},{40,8},{48,16},{56,24},{64,96... | collective-permute-start | bytes 589832 | tf_op jit(solution)/shard_map/ppermute | solution.py:16
  110.5 10.9 %collective-permute-start.9 = (f32[128,3,128]{2,1,0:T(4,128)S(1)}, f32[128,3,128]{2,1,0:T(4,128)S(1)}, u32[]{:S(2)}, u32[]{:S(2)}) collective-permute-start(f32[128,3,128]{2,1,0:T(4,128)S(1)} %get-tuple-element.33), channel_id=1, source_target_pairs={{0,16},{8,24},{16,0},{24,8},{32,48},{40,56},{48,32},{56,40},{64,80... | collective-permute-start | bytes 589832 | tf_op jit(solution)/shard_map/ppermute | solution.py:16
  240.4 5.0 collective-permute-start.12
  241.2 8.4 %collective-permute-start.15 = (f32[128,3,128]{2,1,0:T(4,128)S(1)}, f32[128,3,128]{2,1,0:T(4,128)S(1)}, u32[]{:S(2)}, u32[]{:S(2)}) collective-permute-start(f32[128,3,128]{2,1,0:T(4,128)S(1)} %get-tuple-element.27), channel_id=1, source_target_pairs={{0,1},{1,0},{2,3},{3,2},{4,5},{5,4},{6,7},{7,6},{8,9},{9,8},{10,11... | collective-permute-start | bytes 589832 | tf_op jit(solution)/shard_map/ppermute | solution.py:16
  242.9 9.0 %collective-permute-start.14 = (f32[128,3,128]{2,1,0:T(4,128)S(1)}, f32[128,3,128]{2,1,0:T(4,128)S(1)}, u32[]{:S(2)}, u32[]{:S(2)}) collective-permute-start(f32[128,3,128]{2,1,0:T(4,128)S(1)} %get-tuple-element.28), channel_id=1, source_target_pairs={{0,32},{8,40},{16,48},{24,56},{32,0},{40,8},{48,16},{56,24},{64,96... | collective-permute-start | bytes 589832 | tf_op jit(solution)/shard_map/ppermute | solution.py:16
  244.1 13.0 %collective-permute-start.13 = (f32[128,3,128]{2,1,0:T(4,128)S(1)}, f32[128,3,128]{2,1,0:T(4,128)S(1)}, u32[]{:S(2)}, u32[]{:S(2)}) collective-permute-start(f32[128,3,128]{2,1,0:T(4,128)S(1)} %get-tuple-element.29), channel_id=1, source_target_pairs={{0,16},{8,24},{16,0},{24,8},{32,48},{40,56},{48,32},{56,40},{64,80... | collective-permute-start | bytes 589832 | tf_op jit(solution)/shard_map/ppermute | solution.py:16
  289.4 5.0 collective-permute-start.16
  292.1 7.8 %collective-permute-start.19 = (f32[128,3,128]{2,1,0:T(4,128)S(1)}, f32[128,3,128]{2,1,0:T(4,128)S(1)}, u32[]{:S(2)}, u32[]{:S(2)}) collective-permute-start(f32[128,3,128]{2,1,0:T(4,128)S(1)} %get-tuple-element.23), channel_id=1, source_target_pairs={{0,1},{1,0},{2,3},{3,2},{4,5},{5,4},{6,7},{7,6},{8,9},{9,8},{10,11... | collective-permute-start | bytes 589832 | tf_op jit(solution)/shard_map/ppermute | solution.py:16
  292.4 9.2 %collective-permute-start.18 = (f32[128,3,128]{2,1,0:T(4,128)S(1)}, f32[128,3,128]{2,1,0:T(4,128)S(1)}, u32[]{:S(2)}, u32[]{:S(2)}) collective-permute-start(f32[128,3,128]{2,1,0:T(4,128)S(1)} %get-tuple-element.24), channel_id=1, source_target_pairs={{0,32},{8,40},{16,48},{24,56},{32,0},{40,8},{48,16},{56,24},{64,96... | collective-permute-start | bytes 589832 | tf_op jit(solution)/shard_map/ppermute | solution.py:16
  294.3 11.6 %collective-permute-start.17 = (f32[128,3,128]{2,1,0:T(4,128)S(1)}, f32[128,3,128]{2,1,0:T(4,128)S(1)}, u32[]{:S(2)}, u32[]{:S(2)}) collective-permute-start(f32[128,3,128]{2,1,0:T(4,128)S(1)} %get-tuple-element.25), channel_id=1, source_target_pairs={{0,16},{8,24},{16,0},{24,8},{32,48},{40,56},{48,32},{56,40},{64,80... | collective-permute-start | bytes 589832 | tf_op jit(solution)/shard_map/ppermute | solution.py:16
  416.3 3.7 collective-permute-start.20
  417.3 8.3 %collective-permute-start.23 = (f32[128,3,128]{2,1,0:T(4,128)S(1)}, f32[128,3,128]{2,1,0:T(4,128)S(1)}, u32[]{:S(2)}, u32[]{:S(2)}) collective-permute-start(f32[128,3,128]{2,1,0:T(4,128)S(1)} %get-tuple-element.19), channel_id=1, source_target_pairs={{0,1},{1,0},{2,3},{3,2},{4,5},{5,4},{6,7},{7,6},{8,9},{9,8},{10,11... | collective-permute-start | bytes 589832 | tf_op jit(solution)/shard_map/ppermute | solution.py:16
  419.0 9.0 %collective-permute-start.22 = (f32[128,3,128]{2,1,0:T(4,128)S(1)}, f32[128,3,128]{2,1,0:T(4,128)S(1)}, u32[]{:S(2)}, u32[]{:S(2)}) collective-permute-start(f32[128,3,128]{2,1,0:T(4,128)S(1)} %get-tuple-element.20), channel_id=1, source_target_pairs={{0,32},{8,40},{16,48},{24,56},{32,0},{40,8},{48,16},{56,24},{64,96... | collective-permute-start | bytes 589832 | tf_op jit(solution)/shard_map/ppermute | solution.py:16
  419.9 11.7 %collective-permute-start.21 = (f32[128,3,128]{2,1,0:T(4,128)S(1)}, f32[128,3,128]{2,1,0:T(4,128)S(1)}, u32[]{:S(2)}, u32[]{:S(2)}) collective-permute-start(f32[128,3,128]{2,1,0:T(4,128)S(1)} %get-tuple-element.21), channel_id=1, source_target_pairs={{0,16},{8,24},{16,0},{24,8},{32,48},{40,56},{48,32},{56,40},{64,80... | collective-permute-start | bytes 589832 | tf_op jit(solution)/shard_map/ppermute | solution.py:16
  456.3 0.9 copy-start.1
  466.1 5.8 collective-permute-start.24
  468.8 7.8 %collective-permute-start.27 = (f32[128,3,128]{2,1,0:T(4,128)S(1)}, f32[128,3,128]{2,1,0:T(4,128)S(1)}, u32[]{:S(2)}, u32[]{:S(2)}) collective-permute-start(f32[128,3,128]{2,1,0:T(4,128)S(1)} %get-tuple-element.15), channel_id=1, source_target_pairs={{0,1},{1,0},{2,3},{3,2},{4,5},{5,4},{6,7},{7,6},{8,9},{9,8},{10,11... | collective-permute-start | bytes 589832 | tf_op jit(solution)/shard_map/ppermute | solution.py:16
  469.1 9.0 %collective-permute-start.26 = (f32[128,3,128]{2,1,0:T(4,128)S(1)}, f32[128,3,128]{2,1,0:T(4,128)S(1)}, u32[]{:S(2)}, u32[]{:S(2)}) collective-permute-start(f32[128,3,128]{2,1,0:T(4,128)S(1)} %get-tuple-element.16), channel_id=1, source_target_pairs={{0,32},{8,40},{16,48},{24,56},{32,0},{40,8},{48,16},{56,24},{64,96... | collective-permute-start | bytes 589832 | tf_op jit(solution)/shard_map/ppermute | solution.py:16
  470.8 12.7 %collective-permute-start.25 = (f32[128,3,128]{2,1,0:T(4,128)S(1)}, f32[128,3,128]{2,1,0:T(4,128)S(1)}, u32[]{:S(2)}, u32[]{:S(2)}) collective-permute-start(f32[128,3,128]{2,1,0:T(4,128)S(1)} %get-tuple-element.17), channel_id=1, source_target_pairs={{0,16},{8,24},{16,0},{24,8},{32,48},{40,56},{48,32},{56,40},{64,80... | collective-permute-start | bytes 589832 | tf_op jit(solution)/shard_map/ppermute | solution.py:16
  492.1 90.8 %copy-start.2 = (f32[128,1536]{1,0:T(8,128)S(1)}, f32[128,1536]{1,0:T(8,128)}, u32[]{:S(2)}) copy-start(f32[128,1536]{1,0:T(8,128)} %copy-done.1) | copy-start | bytes 2359300
